TPU v7x, 32 devices: a whole 2x2x4 slice. The times are simulated.
32 devices in a mesh: grp: 2 (over y), col: 4 (over z), row: 2 (over x), limb: 2 (over core).
Axes of the slice: x: 2, y: 2, z: 4, core: 2. Of those that a mesh axis runs over, the one named last changes fastest.
Arguments:
- database: bfloat16 [8192, 8192], P(('grp', 'row'), 'col'), parts along dimension 0, may hold values from -128 to 127, as said below
- lwe_matrix: bfloat16 [8192, 2, 512], P('col', 'limb'), may hold values from -0.0008544922 to 0.0008544922
- secret_ct: float32 [2, 2, 2, 512, 4096], P(None, None, 'limb', 'col', 'row'), may hold values from -6 to 6
Outputs:
- encrypted_product: float32 [4, 2, 4096], P('grp', None, 'row'), parts along dimension 0
There are 2 independent parts, one for each index of `grp`. A program takes and returns all parts, laid end to end along the dimension named above; an argument that names none is the same for every part. Nothing has to cross between parts.
Inputs may be any that keep to these rules, and one draw needn't show every extreme that they name: `database`: whole numbers.
All inputs are finite; a program needn't handle non-finite values.
Results may differ from a plain program's by a relative error of at most 0.0003.
Values sent between devices are 32-bit elements; how exact they have to be, the bound alone decides.
A program may use at most 64 MiB of HBM per device.

v0:
```python
import math
import jax
import jax.numpy as jnp
import numpy as np
from jax import lax
from jax.sharding import PartitionSpec as P

CHUNKS = 4


def tables(row_count, row_dev, fast):
    slow = row_dev // fast
    degree = row_count * row_dev
    m = np.arange(row_dev)
    t = np.arange(fast)
    angle = -2.0 * np.pi * (m[:, None] * t[None, :] % row_dev) / row_dev
    first = np.exp(1j * angle).reshape(fast, slow, fast).transpose(1, 0, 2)
    a = np.arange(row_count)
    n = np.arange(degree)
    turn = -np.pi * (n[None, :] * (2 * a[:, None] + 1) % (2 * degree)) / degree
    turn = np.exp(1j * turn).reshape(row_count, row_count, fast, slow).transpose(0, 3, 1, 2)
    v = np.arange(slow)
    last = np.exp(-2j * np.pi * (v[:, None] * v[None, :] % slow) / slow)
    last = np.stack([np.stack([last.real, last.imag], 0), np.stack([-last.imag, last.real], 0)], 0)
    return (first, turn, last.astype(np.float32))


def body(database, lwe_matrix, secret_ct):
    row_count = lax.axis_size("row")
    row_rank = lax.axis_index("row")
    col_count = lax.axis_size("col")
    row_dev = database.shape[0]
    half = lwe_matrix.shape[2]
    own = half // col_count
    part = own // CHUNKS
    fast = 128
    slow = row_dev // fast
    first, turn, last = tables(row_count, row_dev, fast)
    f_re = jnp.asarray(first.real, jnp.float32)[:, None]
    f_im = jnp.asarray(first.imag, jnp.float32)[:, None]
    g_re = lax.dynamic_index_in_dim(jnp.asarray(turn.real, jnp.float32), row_rank, 0, False)[
        ..., None
    ]
    g_im = lax.dynamic_index_in_dim(jnp.asarray(turn.imag, jnp.float32), row_rank, 0, False)[
        ..., None
    ]
    stage = jnp.stack([f_re * g_re - f_im * g_im, f_re * g_im + f_im * g_re], axis=3)
    stage = stage.reshape(slow, row_count, fast, 2, fast)
    panel = lwe_matrix[:, 0, :].reshape(-1, col_count, own)
    scale = 1.0 / (math.sqrt(row_dev * row_count) * math.sqrt(2 * half))
    prod_real = prod_imag = 0.0
    for k in range(CHUNKS):
        piece = panel[:, :, k * part : (k + 1) * part].reshape(-1, col_count * part)
        partial = lax.dot_general(
            piece, database, (((0,), (1,)), ((), ())), preferred_element_type=jnp.float32
        )
        mine = lax.psum_scatter(partial, "col", scatter_dimension=0, tiled=True)
        blocks = [mine]
        for step in range(1, row_count):
            perm = [(i, (i + step) % row_count) for i in range(row_count)]
            blocks.append(lax.ppermute(mine, "row", perm))
        total = 0.0
        for step, block in enumerate(blocks):
            source = (row_rank - step) % row_count
            table = lax.dynamic_index_in_dim(stage, source, 1, False)
            total = total + jnp.einsum(
                "juv,vuct->vjct",
                block.reshape(part, fast, slow),
                table,
                precision=lax.Precision.HIGH,
                preferred_element_type=jnp.float32,
            )
        spec = jnp.einsum("vjct,cdvs->djst", total, last, precision=lax.Precision.HIGH)
        spec = spec.reshape(2, part, row_dev)
        cipher = secret_ct[:, :, 0, k * part : (k + 1) * part]
        prod_real += jnp.sum(spec[0] * cipher[:, 0] - spec[1] * cipher[:, 1], axis=1)
        prod_imag += jnp.sum(spec[0] * cipher[:, 1] + spec[1] * cipher[:, 0], axis=1)
    return lax.psum(jnp.stack([prod_real, prod_imag], axis=1) * scale, ("col", "limb"))


def solution(mesh):
    placed = (P(("grp", "row"), "col"), P("col", "limb", None), P(None, None, "limb", "col", "row"))
    return jax.shard_map(
        body, mesh=mesh, in_specs=placed, out_specs=P("grp", None, "row"), check_vma=False
    )
```

profile of v0, /device:TPU:0, one launch (start us, length us, event | category | flops | bytes accessed | tf_op | source)
XLA Modules:
  0.0 194.0 jit_solution(14981095304729488325)
XLA Ops:
  6.5 2.9 %copy.16 = bf16[2048,1,512]{0,2,1:T(8,128)(2,1)S(1)} copy(bf16[2048,1,512]{2,0,1:T(8,128)(2,1)} %param.12) | data formatting | bytes 4194304 | tf_op args[1]
  10.5 7.4 %fusion.41 = f32[128,2048]{1,0:T(8,128)} fusion(bf16[2048,128]{0,1:T(8,128)(2,1)S(1)} %bitcast.218, bf16[2048,2048]{1,0:T(8,128)(2,1)} %param.11), kind=kOutput, calls=%fused_computation.88 | convolution fusion | flops 1073741824 | bytes 9961472 | tf_op jit(solution)/shard_map/dot_general | solution.py:54
  18.0 7.2 %fusion.42 = f32[128,2048]{1,0:T(8,128)} fusion(bf16[2048,128]{0,1:T(8,128)(2,1)S(1)} %bitcast.217, bf16[2048,2048]{1,0:T(8,128)(2,1)} %param.11), kind=kOutput, calls=%fused_computation.89 | convolution fusion | flops 1073741824 | bytes 9961472 | tf_op jit(solution)/shard_map/dot_general | solution.py:54
  25.3 7.5 %fusion.43 = f32[128,2048]{1,0:T(8,128)} fusion(bf16[2048,128]{0,1:T(8,128)(2,1)S(1)} %bitcast.216, bf16[2048,2048]{1,0:T(8,128)(2,1)} %param.11), kind=kOutput, calls=%fused_computation.90 | convolution fusion | flops 1073741824 | bytes 9961472 | tf_op jit(solution)/shard_map/dot_general | solution.py:54
  32.9 7.5 %fusion.44 = f32[128,2048]{1,0:T(8,128)} fusion(bf16[2048,128]{0,1:T(8,128)(2,1)S(1)} %bitcast.215, bf16[2048,2048]{1,0:T(8,128)(2,1)} %param.11), kind=kOutput, calls=%fused_computation.91 | convolution fusion | flops 1073741824 | bytes 9961472 | tf_op jit(solution)/shard_map/dot_general | solution.py:54
  40.4 10.7 %multiply_add_fusion = (f32[16,2,128,1,128]{4,3,2,1,0:T(1,128)}, f32[16,2,128,1,128]{4,3,2,1,0:T(1,128)}) fusion(f32[16,2,128]{2,1,0:T(2,128)S(1)} %dynamic-slice_bitcast_fusion, f32[16,128,128]{2,1,0:T(8,128)S(1)} %copy-done.23, f32[16,2,128]{2,1,0:T(2,128)S(1)} %dynamic-slice_bitcast_fusion.1, f32[16,128,128]{2,1,0:T(8,128)S(1)} %copy-done.22), kind=kLoop, calls=%fused_computation.8 | loop fusion | flops 3145728 | bytes 6324224 | tf_op jit(solution)/shard_map/add | solution.py:47
  51.2 6.5 %fusion.3 = (f32[16,128,2,128]{3,2,1,0:T(2,128)}, f32[16,128,2,128]{3,2,1,0:T(2,128)S(1)}) fusion(s32[]{:T(128)S(6)} %select_n.43, f32[16,2,128,1,128]{4,3,2,1,0:T(1,128)} %get-tuple-element.20, f32[16,2,128,1,128]{4,3,2,1,0:T(1,128)} %get-tuple-element.19, s32[]{:T(128)S(6)} %select_n.45), kind=kLoop, calls=%fused_computation.7 | loop fusion | flops 1048576 | bytes 8388616 | tf_op jit(solution)/shard_map/jit(dynamic_index_in_dim)/squeeze | solution.py:65
  57.7 2.1 %slice_bitcast_fusion.2 = (f32[2,2,32,2048]{3,2,1,0:T(8,128)}, f32[2,2,32,2048]{3,2,1,0:T(8,128)}, f32[2,2,32,2048]{3,2,1,0:T(8,128)}, f32[2,2,32,2048]{3,2,1,0:T(8,128)}) fusion(f32[2,2,1,128,2048]{4,3,2,1,0:T(8,128)S(1)} %copy-done.3), kind=kLoop, calls=%fused_computation.40 | loop fusion | bytes 8388608 | tf_op jit(solution)/shard_map/squeeze | solution.py:75
  59.7 2.8 %collective-permute-start = (f32[32,2048]{1,0:T(8,128)}, f32[32,2048]{1,0:T(8,128)}, u32[]{:S(2)}, u32[]{:S(2)}) collective-permute-start(f32[32,2048]{1,0:T(8,128)} %reduce-scatter.5.cloned.1.call-done), channel_id=1, source_target_pairs={{0,2},{2,0},{1,3},{3,1},{4,6},{6,4},{5,7},{7,5},{8,10},{10,8},{9,1... | collective-permute-start | bytes 786440 | tf_op jit(solution)/shard_map/ppermute | solution.py:61
  63.9 12.3 %reduce-scatter.7.cloned.1.call-done = f32[32,2048]{1,0:T(8,128)} async-done(((f32[128,2048]{1,0:T(8,128)}), f32[32,2048]{1,0:T(8,128)}) %reduce-scatter.7.cloned.1.call-update) | async-done | bytes 262160 | tf_op jit(solution)/shard_map/reduce_scatter | solution.py:57
  76.2 1.5 collective-permute-start.1
  77.7 2.4 %copy.20 = f32[32,2048]{0,1:T(8,128)} copy(f32[32,2048]{1,0:T(8,128)} %reduce-scatter.7.cloned.1.call-done) | data formatting | bytes 524288 | tf_op jit(solution)/shard_map/reduce_scatter | solution.py:57
  80.1 24.2 %reduce-scatter.9.cloned.1.call-done = f32[32,2048]{1,0:T(8,128)} async-done(((f32[128,2048]{1,0:T(8,128)}), f32[32,2048]{1,0:T(8,128)}) %reduce-scatter.9.cloned.1.call-update) | async-done | bytes 262160 | tf_op jit(solution)/shard_map/reduce_scatter | solution.py:57
  104.3 1.5 collective-permute-start.2
  105.8 2.3 %copy.23 = f32[32,2048]{0,1:T(8,128)} copy(f32[32,2048]{1,0:T(8,128)} %reduce-scatter.9.cloned.1.call-done) | data formatting | bytes 524288 | tf_op jit(solution)/shard_map/reduce_scatter | solution.py:57
  108.1 3.8 %fusion.18 = f32[16,32,2,128]{3,1,2,0:T(8,128)} fusion(f32[16,128,2,128]{3,2,1,0:T(2,128)} %get-tuple-element.17, f32[32,128,16,1]{0,2,1,3:T(8,128)S(1)} %bitcast.207), kind=kOutput, calls=%fused_computation.24 | convolution fusion | flops 100663296 | bytes 2883584 | tf_op jit(solution)/shard_map/juv,vuct->vjct/dot_general | solution.py:66
  112.0 2.2 %fusion.16 = f32[16,32,2,128]{3,1,2,0:T(8,128)} fusion(f32[16,128,2,128]{3,2,1,0:T(2,128)S(1)} %copy-done, f32[32,128,16,1]{0,2,1,3:T(8,128)S(1)} %bitcast.208), kind=kOutput, calls=%fused_computation.22 | convolution fusion | flops 100663296 | bytes 2883584 | tf_op jit(solution)/shard_map/juv,vuct->vjct/dot_general | solution.py:66
  114.2 2.2 %fusion.14 = f32[16,32,2,128]{3,1,2,0:T(8,128)} fusion(f32[16,128,2,128]{3,2,1,0:T(2,128)S(1)} %copy-done, f32[32,128,16,1]{0,2,1,3:T(8,128)S(1)} %bitcast.209), kind=kOutput, calls=%fused_computation.20 | convolution fusion | flops 100663296 | bytes 2883584 | tf_op jit(solution)/shard_map/juv,vuct->vjct/dot_general | solution.py:66
  116.4 15.8 %reduce-scatter.11.cloned.1.call-done = f32[32,2048]{1,0:T(8,128)} async-done(((f32[128,2048]{1,0:T(8,128)}), f32[32,2048]{1,0:T(8,128)}) %reduce-scatter.11.cloned.1.call-update) | async-done | bytes 262160 | tf_op jit(solution)/shard_map/reduce_scatter | solution.py:57
  132.3 1.5 collective-permute-start.3
  135.1 3.7 %fusion.12 = f32[16,32,2,128]{3,1,2,0:T(8,128)} fusion(f32[16,128,2,128]{3,2,1,0:T(2,128)} %get-tuple-element.17, f32[32,128,16,1]{0,2,1,3:T(8,128)S(1)} %bitcast.212), kind=kOutput, calls=%fused_computation.18 | convolution fusion | flops 100663296 | bytes 2883584 | tf_op jit(solution)/shard_map/juv,vuct->vjct/dot_general | solution.py:66
  140.1 1.3 fusion.10
  148.0 1.5 fusion.6
  160.8 25.9 %psum.7 = f32[2,2,2048]{2,0,1:T(2,128)S(1)} all-reduce(f32[2,2,2048]{2,0,1:T(2,128)S(1)} %maximum_multiply_fusion), channel_id=1, replica_groups=mesh['grp'=2,'col'=4,'row'=2,'limb'=2] {'col','limb'}, use_global_device_ids=true, to_apply=%region_12.13 | all-reduce | flops 8192 | bytes 65536 | tf_op jit(solution)/shard_map/psum | solution.py:78
  (100 shorter events, 23.4 us)
Async XLA Ops:
  6.5 53.2 %reduce-scatter.5.cloned.1.call-start = ((), (), s32[]{:S(2)}) async-start(), calls=%async_computation.4 | async-start | bytes 1310720 | tf_op jit(solution)/shard_map/reduce_scatter | solution.py:57
  10.5 7.5 %copy-start.12 = (bf16[2048,4,32]{0,2,1:T(8,128)(2,1)S(1)}, bf16[2048,4,32]{0,2,1:T(8,128)(2,1)}, u32[]{:S(2)}) copy-start(bf16[2048,4,32]{0,2,1:T(8,128)(2,1)} %get-tuple-element.21) | copy-start | bytes 1572868
  17.9 58.3 %reduce-scatter.7.cloned.1.call-start = ((), (), s32[]{:S(2)}) async-start(), calls=%async_computation.5 | async-start | bytes 1310720 | tf_op jit(solution)/shard_map/reduce_scatter | solution.py:57
  25.2 79.1 %reduce-scatter.9.cloned.1.call-start = ((), (), s32[]{:S(2)}) async-start(), calls=%async_computation.6 | async-start | bytes 1310720 | tf_op jit(solution)/shard_map/reduce_scatter | solution.py:57
  32.8 99.5 %reduce-scatter.11.cloned.1.call-start = ((), (), s32[]{:S(2)}) async-start(), calls=%async_computation.7 | async-start | bytes 1310720 | tf_op jit(solution)/shard_map/reduce_scatter | solution.py:57
  32.8 7.5 %copy-start.26 = (f32[2,16,2,128]{3,2,1,0:T(2,128)S(1)}, f32[2,16,2,128]{3,2,1,0:T(2,128)}, u32[]{:S(2)}) copy-start(f32[2,16,2,128]{3,2,1,0:T(2,128)} %constant.77.clone) | copy-start | bytes 98308
  32.8 7.6 %copy-start.25 = (f32[2,16,2,128]{3,2,1,0:T(2,128)S(1)}, f32[2,16,2,128]{3,2,1,0:T(2,128)}, u32[]{:S(2)}) copy-start(f32[2,16,2,128]{3,2,1,0:T(2,128)} %constant.76.clone) | copy-start | bytes 98308
  32.8 7.6 %copy-start.22 = (f32[16,128,128]{2,1,0:T(8,128)S(1)}, f32[16,128,128]{2,1,0:T(8,128)}, u32[]{:S(2)}) copy-start(f32[16,128,128]{2,1,0:T(8,128)} %constant.74.clone) | copy-start | bytes 3145732
  32.9 7.6 %copy-start.23 = (f32[16,128,128]{2,1,0:T(8,128)S(1)}, f32[16,128,128]{2,1,0:T(8,128)}, u32[]{:S(2)}) copy-start(f32[16,128,128]{2,1,0:T(8,128)} %constant.75.clone) | copy-start | bytes 3145732
  51.2 6.5 %copy-start.3 = (f32[2,2,1,128,2048]{4,3,2,1,0:T(8,128)S(1)}, f32[2,2,1,128,2048]{4,3,2,1,0:T(8,128)}, u32[]{:S(2)}) copy-start(f32[2,2,1,128,2048]{4,3,2,1,0:T(8,128)} %param.13) | copy-start | bytes 12582916
  59.7 79.0 %collective-permute-start = (f32[32,2048]{1,0:T(8,128)}, f32[32,2048]{1,0:T(8,128)}, u32[]{:S(2)}, u32[]{:S(2)}) collective-permute-start(f32[32,2048]{1,0:T(8,128)} %reduce-scatter.5.cloned.1.call-done), channel_id=1, source_target_pairs={{0,2},{2,0},{1,3},{3,1},{4,6},{6,4},{5,7},{7,5},{8,10},{10,8},{9,1... | collective-permute-start | bytes 786440 | tf_op jit(solution)/shard_map/ppermute | solution.py:61
  76.2 67.1 %collective-permute-start.1 = (f32[32,2048]{1,0:T(8,128)}, f32[32,2048]{1,0:T(8,128)}, u32[]{:S(2)}, u32[]{:S(2)}) collective-permute-start(f32[32,2048]{1,0:T(8,128)} %reduce-scatter.7.cloned.1.call-done), channel_id=1, source_target_pairs={{0,2},{2,0},{1,3},{3,1},{4,6},{6,4},{5,7},{7,5},{8,10},{10,8},{9,1... | collective-permute-start | bytes 786440 | tf_op jit(solution)/shard_map/ppermute | solution.py:61
  104.3 43.4 %collective-permute-start.2 = (f32[32,2048]{1,0:T(8,128)}, f32[32,2048]{1,0:T(8,128)S(1)}, u32[]{:S(2)}, u32[]{:S(2)}) collective-permute-start(f32[32,2048]{1,0:T(8,128)} %reduce-scatter.9.cloned.1.call-done), channel_id=1, source_target_pairs={{0,2},{2,0},{1,3},{3,1},{4,6},{6,4},{5,7},{7,5},{8,10},{10,8},{9,1... | collective-permute-start | bytes 786440 | tf_op jit(solution)/shard_map/ppermute | solution.py:61
  108.1 3.8 %copy-start = (f32[16,128,2,128]{3,2,1,0:T(2,128)S(1)}, f32[16,128,2,128]{3,2,1,0:T(2,128)}, u32[]{:S(2)}) copy-start(f32[16,128,2,128]{3,2,1,0:T(2,128)} %get-tuple-element.17) | copy-start | bytes 6291460
  108.1 3.8 %copy-start.1 = (f32[32,2048]{0,1:T(8,128)S(1)}, f32[32,2048]{0,1:T(8,128)}, u32[]{:S(2)}) copy-start(f32[32,2048]{0,1:T(8,128)} %copy.20) | copy-start | bytes 786436
  111.9 2.3 %copy-start.2 = (f32[32,2048]{0,1:T(8,128)S(1)}, f32[32,2048]{0,1:T(8,128)}, u32[]{:S(2)}) copy-start(f32[32,2048]{0,1:T(8,128)} %copy.23) | copy-start | bytes 786436
  132.3 22.5 %collective-permute-start.3 = (f32[32,2048]{1,0:T(8,128)}, f32[32,2048]{1,0:T(8,128)}, u32[]{:S(2)}, u32[]{:S(2)}) collective-permute-start(f32[32,2048]{1,0:T(8,128)} %reduce-scatter.11.cloned.1.call-done), channel_id=1, source_target_pairs={{0,2},{2,0},{1,3},{3,1},{4,6},{6,4},{5,7},{7,5},{8,10},{10,8},{9,1... | collective-permute-start | bytes 786440 | tf_op jit(solution)/shard_map/ppermute | solution.py:61
  148.0 2.6 %copy-start.19 = (f32[1,32,16,128]{3,2,0,1:T(8,128)S(1)}, f32[1,32,16,128]{3,2,0,1:T(8,128)}, u32[]{:S(2)}) copy-start(f32[1,32,16,128]{3,2,0,1:T(8,128)} %get-tuple-element.28) | copy-start | bytes 786436
  148.0 2.7 %copy-start.18 = (f32[1,32,16,128]{3,2,0,1:T(8,128)S(1)}, f32[1,32,16,128]{3,2,0,1:T(8,128)}, u32[]{:S(2)}) copy-start(f32[1,32,16,128]{3,2,0,1:T(8,128)} %get-tuple-element.27) | copy-start | bytes 786436
  149.6 1.9 copy-start.21
  149.6 2.7 %copy-start.20 = (f32[1,32,16,128]{3,2,0,1:T(8,128)S(1)}, f32[1,32,16,128]{3,2,0,1:T(8,128)}, u32[]{:S(2)}) copy-start(f32[1,32,16,128]{3,2,0,1:T(8,128)} %get-tuple-element.25) | copy-start | bytes 786436
  158.5 1.7 copy-start.5
  158.5 1.7 copy-start.14
  158.5 1.8 copy-start.16
  (11 other events, 16.0 us)
Sparse Core Ops, SparseCore 0:
  18.0 29.9 reduce-scatter.4
  50.4 25.7 reduce-scatter.6
  78.5 25.7 reduce-scatter.8
  106.4 25.7 reduce-scatter.10
where the time goes:
time: 195 us; the launch traced here: 194 us
  waiting for transfers between devices  52.5 us (27%)
  matrix products  50.9 us (26%)
  blocking collectives  25.9 us (13%)
  local copies, waits for them, and re-layouts  25.3 us (13%)
  other arithmetic  18.3 us (9%)
  between operations  13.6 us (7%)
  starting transfers between devices  7.37 us (4%)
    reduce_scatter x4, waiting for transfers between devices, body(): mine = lax.psum_scatter(partial, 'col', scatter_dimension=0, tiled=True)  52.4 us
    dot_general x4, matrix products, body(): lax.dot_general(piece, database, (((0,), (1,)), ((), ())), preferred_elem...  29.6 us
    psum x1, blocking collectives, body(): lax.psum(jnp.stack([prod_real, prod_imag], axis=1) * scale, ('col', 'limb'))  25.9 us
    dot_general x8, matrix products, body(): jnp.einsum('juv,vuct->vjct', block.reshape(part, fast, slow), table, prec...  17.5 us
    add x1, other arithmetic, body(): f_re * g_im + f_im * g_re  10.7 us
    unnamed x63, local copies, waits for them, and re-layouts  8.37 us
    reduce_scatter x4, local copies, waits for them, and re-layouts, body(): mine = lax.psum_scatter(partial, 'col', scatter_dimension=0, tiled=True)  7.35 us
    ppermute x4, starting transfers between devices, body(): blocks.append(lax.ppermute(mine, 'row', perm))  7.24 us
  transfers between devices with their start and end apart: 8, of which 3 were waited for; matrix products, arithmetic and copies ran while one was open for 39% of the time, Pallas kernels for 0%

commit v1 on v0

--- a/solution.py
+++ b/solution.py
@@ -75,7 +75,9 @@
         cipher = secret_ct[:, :, 0, k * part : (k + 1) * part]
         prod_real += jnp.sum(spec[0] * cipher[:, 0] - spec[1] * cipher[:, 1], axis=1)
         prod_imag += jnp.sum(spec[0] * cipher[:, 1] + spec[1] * cipher[:, 0], axis=1)
-    return lax.psum(jnp.stack([prod_real, prod_imag], axis=1) * scale, ("col", "limb"))
+    return jnp.sum(
+        lax.all_gather(jnp.stack([prod_real, prod_imag], axis=1) * scale, ("col", "limb")), axis=0
+    )
 
 
 def solution(mesh):

time: 195 us -> 185 us (0.949)
  waiting for transfers between devices: 52.5 us -> 68.5 us
  other arithmetic: 18.3 us -> 4.91 us
  blocking collectives: 25.9 us -> 14.2 us
    psum x1 -> x0, blocking collectives: 25.9 us -> none  [body(): lax.psum(jnp.stack([prod_real, prod_imag], axis=1) * scale, ('col', 'limb'))]
    reduce_scatter x4, waiting for transfers between devices: 52.4 us -> 68.4 us  [body(): mine = lax.psum_scatter(partial, 'col', scatter_dimension=0, tiled=True)]
    all_gather x0 -> x1, blocking collectives: none -> 14.2 us  [body(): lax.all_gather(jnp.stack([prod_real, prod_imag], axis=1) * scale, ('col',...]
    add x1, other arithmetic: 10.7 us -> 1.43 us  [body(): f_re * g_im + f_im * g_re]
    squeeze x1, other arithmetic: 6.51 us -> 1.72 us  [body(): table = lax.dynamic_index_in_dim(stage, source, 1, False)]
    unnamed x63 -> x55, local copies, waits for them, and re-layouts: 8.37 us -> 9.68 us
  transfers between devices with their start and end apart: 8 -> 8, of which waited for: 3 -> 4; matrix products, arithmetic and copies ran while one was open for 39% -> 33% of each run, Pallas kernels for 0% -> 0%
where the time goes in v1:
time: 185 us; the launch traced here: 184 us
  waiting for transfers between devices  68.5 us (37%)
  matrix products  50.5 us (27%)
  local copies, waits for them, and re-layouts  26 us (14%)
  blocking collectives  14.2 us (8%)
  between operations  13.6 us (7%)
  starting transfers between devices  6.43 us (3%)
  other arithmetic  4.91 us (3%)
    reduce_scatter x4, waiting for transfers between devices, body(): mine = lax.psum_scatter(partial, 'col', scatter_dimension=0, tiled=True)  68.4 us
    dot_general x4, matrix products, body(): lax.dot_general(piece, database, (((0,), (1,)), ((), ())), preferred_elem...  29.6 us
    dot_general x8, matrix products, body(): jnp.einsum('juv,vuct->vjct', block.reshape(part, fast, slow), table, prec...  18.1 us
    all_gather x1, blocking collectives, body(): lax.all_gather(jnp.stack([prod_real, prod_imag], axis=1) * scale, ('col',...  14.2 us
    unnamed x55, local copies, waits for them, and re-layouts  9.68 us
    reduce_scatter x4, local copies, waits for them, and re-layouts, body(): mine = lax.psum_scatter(partial, 'col', scatter_dimension=0, tiled=True)  7.22 us
    ppermute x4, starting transfers between devices, body(): blocks.append(lax.ppermute(mine, 'row', perm))  6.3 us
    ppermute x4, local copies, waits for them, and re-layouts, body(): blocks.append(lax.ppermute(mine, 'row', perm))  4.16 us
  transfers between devices with their start and end apart: 8, of which 4 were waited for; matrix products, arithmetic and copies ran while one was open for 33% of the time, Pallas kernels for 0%

profile of v1, /device:TPU:0, one launch (start us, length us, event | category | flops | bytes accessed | tf_op | source)
XLA Modules:
  0.0 184.1 jit_solution(11759244660045205626)
XLA Ops:
  6.5 2.9 %copy.29 = bf16[2048,1,512]{0,2,1:T(8,128)(2,1)S(1)} copy(bf16[2048,1,512]{2,0,1:T(8,128)(2,1)} %param.12) | data formatting | bytes 4194304 | tf_op args[1]
  10.5 7.4 %fusion.29 = f32[128,2048]{1,0:T(8,128)} fusion(bf16[2048,128]{0,1:T(8,128)(2,1)S(1)} %bitcast.210, bf16[2048,2048]{1,0:T(8,128)(2,1)} %param.11), kind=kOutput, calls=%fused_computation.76 | convolution fusion | flops 1073741824 | bytes 9961472 | tf_op jit(solution)/shard_map/dot_general | solution.py:54
  18.0 7.2 %fusion.30 = f32[128,2048]{1,0:T(8,128)} fusion(bf16[2048,128]{0,1:T(8,128)(2,1)S(1)} %bitcast.209, bf16[2048,2048]{1,0:T(8,128)(2,1)} %param.11), kind=kOutput, calls=%fused_computation.77 | convolution fusion | flops 1073741824 | bytes 9961472 | tf_op jit(solution)/shard_map/dot_general | solution.py:54
  25.3 7.5 %fusion.31 = f32[128,2048]{1,0:T(8,128)} fusion(bf16[2048,128]{0,1:T(8,128)(2,1)S(1)} %bitcast.208, bf16[2048,2048]{1,0:T(8,128)(2,1)} %param.11), kind=kOutput, calls=%fused_computation.78 | convolution fusion | flops 1073741824 | bytes 9961472 | tf_op jit(solution)/shard_map/dot_general | solution.py:54
  32.9 7.4 %fusion.32 = f32[128,2048]{1,0:T(8,128)} fusion(bf16[2048,128]{0,1:T(8,128)(2,1)S(1)} %bitcast.207, bf16[2048,2048]{1,0:T(8,128)(2,1)} %param.11), kind=kOutput, calls=%fused_computation.79 | convolution fusion | flops 1073741824 | bytes 9961472 | tf_op jit(solution)/shard_map/dot_general | solution.py:54
  41.9 1.7 fusion.1
  44.9 2.1 %slice_bitcast_fusion.2 = (f32[2,2,32,2048]{3,2,1,0:T(8,128)}, f32[2,2,32,2048]{3,2,1,0:T(8,128)}, f32[2,2,32,2048]{3,2,1,0:T(8,128)}, f32[2,2,32,2048]{3,2,1,0:T(8,128)}) fusion(f32[2,2,1,128,2048]{4,3,2,1,0:T(8,128)S(1)} %copy-done.3), kind=kLoop, calls=%fused_computation.36 | loop fusion | bytes 8388608 | tf_op jit(solution)/shard_map/squeeze | solution.py:75
  49.3 1.8 collective-permute-start
  51.1 25.0 %reduce-scatter.7.cloned.1.call-done = f32[32,2048]{1,0:T(8,128)} async-done(((f32[128,2048]{1,0:T(8,128)}), f32[32,2048]{1,0:T(8,128)}) %reduce-scatter.7.cloned.1.call-update) | async-done | bytes 262160 | tf_op jit(solution)/shard_map/reduce_scatter | solution.py:57
  76.2 2.4 %copy.36 = f32[32,2048]{0,1:T(8,128)} copy(f32[32,2048]{1,0:T(8,128)} %reduce-scatter.7.cloned.1.call-done) | data formatting | bytes 524288 | tf_op jit(solution)/shard_map/reduce_scatter | solution.py:57
  78.5 1.5 collective-permute-start.1
  80.0 24.3 %reduce-scatter.9.cloned.1.call-done = f32[32,2048]{1,0:T(8,128)} async-done(((f32[128,2048]{1,0:T(8,128)}), f32[32,2048]{1,0:T(8,128)}) %reduce-scatter.9.cloned.1.call-update) | async-done | bytes 262160 | tf_op jit(solution)/shard_map/reduce_scatter | solution.py:57
  104.3 2.3 %copy.42 = f32[32,2048]{0,1:T(8,128)} copy(f32[32,2048]{1,0:T(8,128)} %reduce-scatter.9.cloned.1.call-done) | data formatting | bytes 524288 | tf_op jit(solution)/shard_map/reduce_scatter | solution.py:57
  108.1 2.0 %fusion.18 = f32[16,32,2,128]{3,1,2,0:T(8,128)} fusion(f32[16,128,2,128]{3,1,2,0:T(8,128)S(1)} %get-tuple-element.18, f32[32,128,16,1]{0,2,1,3:T(8,128)S(1)} %bitcast.199), kind=kOutput, calls=%fused_computation.32 | convolution fusion | flops 100663296 | bytes 2883584 | tf_op jit(solution)/shard_map/juv,vuct->vjct/dot_general | solution.py:66
  110.2 2.1 %fusion.15 = f32[16,32,2,128]{3,1,2,0:T(8,128)} fusion(f32[16,128,2,128]{3,1,2,0:T(8,128)S(1)} %get-tuple-element.18, f32[32,128,16,1]{0,2,1,3:T(8,128)S(1)} %bitcast.200), kind=kOutput, calls=%fused_computation.29 | convolution fusion | flops 100663296 | bytes 2883584 | tf_op jit(solution)/shard_map/juv,vuct->vjct/dot_general | solution.py:66
  112.3 2.1 %fusion.12 = f32[16,32,2,128]{3,1,2,0:T(8,128)} fusion(f32[16,128,2,128]{3,1,2,0:T(8,128)S(1)} %get-tuple-element.18, f32[32,128,16,1]{0,2,1,3:T(8,128)S(1)} %bitcast.201), kind=kOutput, calls=%fused_computation.26 | convolution fusion | flops 100663296 | bytes 2883584 | tf_op jit(solution)/shard_map/juv,vuct->vjct/dot_general | solution.py:66
  114.3 17.9 %reduce-scatter.11.cloned.1.call-done = f32[32,2048]{1,0:T(8,128)} async-done(((f32[128,2048]{1,0:T(8,128)}), f32[32,2048]{1,0:T(8,128)}) %reduce-scatter.11.cloned.1.call-update) | async-done | bytes 262160 | tf_op jit(solution)/shard_map/reduce_scatter | solution.py:57
  133.6 1.5 collective-permute-start.3
  135.1 2.1 %fusion.9 = f32[16,32,2,128]{3,1,2,0:T(8,128)} fusion(f32[16,128,2,128]{3,1,2,0:T(8,128)S(1)} %get-tuple-element.18, f32[32,128,16,1]{0,2,1,3:T(8,128)S(1)} %bitcast.202), kind=kOutput, calls=%fused_computation.23 | convolution fusion | flops 100663296 | bytes 2883584 | tf_op jit(solution)/shard_map/juv,vuct->vjct/dot_general | solution.py:66
  138.5 2.9 %fusion.7 = f32[16,32,2,128,1]{3,1,2,0,4:T(8,128)S(1)} fusion(f32[16,32,2,128]{3,1,2,0:T(8,128)} %fusion.18, f32[16,128,2,128]{3,1,2,0:T(8,128)} %get-tuple-element.17, f32[32,128,16,1]{0,2,1,3:T(8,128)S(1)} %bitcast.203), kind=kOutput, calls=%fused_computation.17 | convolution fusion | flops 100794368 | bytes 3407872 | tf_op jit(solution)/shard_map/juv,vuct->vjct/dot_general | solution.py:66
  144.2 2.3 %fusion.6 = f32[16,32,2,128,1]{3,1,2,0,4:T(8,128)S(1)} fusion(f32[16,32,2,128]{3,1,2,0:T(8,128)} %fusion.15, f32[16,128,2,128]{3,1,2,0:T(8,128)S(1)} %copy-done, f32[32,128,16,1]{0,2,1,3:T(8,128)S(1)} %bitcast.205), kind=kOutput, calls=%fused_computation.15 | convolution fusion | flops 100794368 | bytes 3407872 | tf_op jit(solution)/shard_map/juv,vuct->vjct/dot_general | solution.py:66
  148.4 2.4 %fusion.5 = f32[16,32,2,128,1]{3,1,2,0,4:T(8,128)S(1)} fusion(f32[16,32,2,128]{3,1,2,0:T(8,128)} %fusion.12, f32[16,128,2,128]{3,1,2,0:T(8,128)S(1)} %copy-done, f32[32,128,16,1]{0,2,1,3:T(8,128)S(1)} %bitcast.206), kind=kOutput, calls=%fused_computation.13 | convolution fusion | flops 100794368 | bytes 3407872 | tf_op jit(solution)/shard_map/juv,vuct->vjct/dot_general | solution.py:66
  157.0 2.3 %fusion.4 = f32[16,32,2,128,1]{3,1,2,0,4:T(8,128)S(1)} fusion(f32[16,32,2,128]{3,1,2,0:T(8,128)} %fusion.9, f32[16,128,2,128]{3,1,2,0:T(8,128)S(1)} %copy-done, f32[32,128,16,1]{0,2,1,3:T(8,128)S(1)} %bitcast.204), kind=kOutput, calls=%fused_computation.11 | convolution fusion | flops 100794368 | bytes 3407872 | tf_op jit(solution)/shard_map/juv,vuct->vjct/dot_general | solution.py:66
  162.7 14.2 %all_gather.4 = f32[8,2,2,2048]{3,2,1,0:T(2,128)S(1)} all-gather(f32[1,2,2,2048]{3,2,1,0:T(2,128)S(1)} %maximum_multiply_fusion), channel_id=1, replica_groups=mesh['grp'=2,'col'=4,'row'=2,'limb'=2] {'col','limb'}, dimensions={0}, use_global_device_ids=true | all-gather | bytes 294912 | tf_op jit(solution)/shard_map/all_gather | solution.py:79
  (94 shorter events, 25.1 us)
Async XLA Ops:
  6.5 41.5 %reduce-scatter.5.cloned.1.call-start = ((), (), s32[]{:S(2)}) async-start(), calls=%async_computation.4 | async-start | bytes 1310720 | tf_op jit(solution)/shard_map/reduce_scatter | solution.py:57
  10.5 7.5 %copy-start.8 = (bf16[2048,4,32]{0,2,1:T(8,128)(2,1)S(1)}, bf16[2048,4,32]{0,2,1:T(8,128)(2,1)}, u32[]{:S(2)}) copy-start(bf16[2048,4,32]{0,2,1:T(8,128)(2,1)} %get-tuple-element.21) | copy-start | bytes 1572868
  17.9 58.3 %reduce-scatter.7.cloned.1.call-start = ((), (), s32[]{:S(2)}) async-start(), calls=%async_computation.5 | async-start | bytes 1310720 | tf_op jit(solution)/shard_map/reduce_scatter | solution.py:57
  25.2 79.1 %reduce-scatter.9.cloned.1.call-start = ((), (), s32[]{:S(2)}) async-start(), calls=%async_computation.6 | async-start | bytes 1310720 | tf_op jit(solution)/shard_map/reduce_scatter | solution.py:57
  32.8 99.5 %reduce-scatter.11.cloned.1.call-start = ((), (), s32[]{:S(2)}) async-start(), calls=%async_computation.7 | async-start | bytes 1310720 | tf_op jit(solution)/shard_map/reduce_scatter | solution.py:57
  32.8 7.6 %copy-start.22 = (f32[2,16,2,128]{3,1,2,0:T(8,128)S(1)}, f32[2,16,2,128]{3,1,2,0:T(8,128)}, u32[]{:S(2)}) copy-start(f32[2,16,2,128]{3,1,2,0:T(8,128)} %constant.77.clone) | copy-start | bytes 98308
  32.8 7.6 %copy-start.21 = (f32[2,16,2,128]{3,1,2,0:T(8,128)S(1)}, f32[2,16,2,128]{3,1,2,0:T(8,128)}, u32[]{:S(2)}) copy-start(f32[2,16,2,128]{3,1,2,0:T(8,128)} %constant.76.clone) | copy-start | bytes 98308
  32.8 7.6 %copy-start.18 = (f32[16,128,128]{2,1,0:T(8,128)S(1)}, f32[16,128,128]{2,1,0:T(8,128)}, u32[]{:S(2)}) copy-start(f32[16,128,128]{2,1,0:T(8,128)} %constant.74.clone) | copy-start | bytes 3145732
  32.9 7.6 %copy-start.19 = (f32[16,128,128]{2,1,0:T(8,128)S(1)}, f32[16,128,128]{2,1,0:T(8,128)}, u32[]{:S(2)}) copy-start(f32[16,128,128]{2,1,0:T(8,128)} %constant.75.clone) | copy-start | bytes 3145732
  41.9 3.0 %copy-start.3 = (f32[2,2,1,128,2048]{4,3,2,1,0:T(8,128)S(1)}, f32[2,2,1,128,2048]{4,3,2,1,0:T(8,128)}, u32[]{:S(2)}) copy-start(f32[2,2,1,128,2048]{4,3,2,1,0:T(8,128)} %param.13) | copy-start | bytes 12582916
  49.3 87.8 %collective-permute-start = (f32[32,2048]{1,0:T(8,128)}, f32[32,2048]{1,0:T(8,128)}, u32[]{:S(2)}, u32[]{:S(2)}) collective-permute-start(f32[32,2048]{1,0:T(8,128)} %reduce-scatter.5.cloned.1.call-done), channel_id=1, source_target_pairs={{0,2},{2,0},{1,3},{3,1},{4,6},{6,4},{5,7},{7,5},{8,10},{10,8},{9,1... | collective-permute-start | bytes 786440 | tf_op jit(solution)/shard_map/ppermute | solution.py:61
  78.5 64.4 %collective-permute-start.1 = (f32[32,2048]{1,0:T(8,128)}, f32[32,2048]{1,0:T(8,128)}, u32[]{:S(2)}, u32[]{:S(2)}) collective-permute-start(f32[32,2048]{1,0:T(8,128)} %reduce-scatter.7.cloned.1.call-done), channel_id=1, source_target_pairs={{0,2},{2,0},{1,3},{3,1},{4,6},{6,4},{5,7},{7,5},{8,10},{10,8},{9,1... | collective-permute-start | bytes 786440 | tf_op jit(solution)/shard_map/ppermute | solution.py:61
  106.6 3.5 %copy-start.1 = (f32[32,2048]{0,1:T(8,128)S(1)}, f32[32,2048]{0,1:T(8,128)}, u32[]{:S(2)}) copy-start(f32[32,2048]{0,1:T(8,128)} %copy.36) | copy-start | bytes 786436
  106.6 41.4 %collective-permute-start.2 = (f32[32,2048]{1,0:T(8,128)}, f32[32,2048]{1,0:T(8,128)S(1)}, u32[]{:S(2)}, u32[]{:S(2)}) collective-permute-start(f32[32,2048]{1,0:T(8,128)} %reduce-scatter.9.cloned.1.call-done), channel_id=1, source_target_pairs={{0,2},{2,0},{1,3},{3,1},{4,6},{6,4},{5,7},{7,5},{8,10},{10,8},{9,1... | collective-permute-start | bytes 786440 | tf_op jit(solution)/shard_map/ppermute | solution.py:61
  110.2 2.1 %copy-start.2 = (f32[32,2048]{0,1:T(8,128)S(1)}, f32[32,2048]{0,1:T(8,128)}, u32[]{:S(2)}) copy-start(f32[32,2048]{0,1:T(8,128)} %copy.42) | copy-start | bytes 786436
  133.6 22.2 %collective-permute-start.3 = (f32[32,2048]{1,0:T(8,128)}, f32[32,2048]{1,0:T(8,128)}, u32[]{:S(2)}, u32[]{:S(2)}) collective-permute-start(f32[32,2048]{1,0:T(8,128)} %reduce-scatter.11.cloned.1.call-done), channel_id=1, source_target_pairs={{0,2},{2,0},{1,3},{3,1},{4,6},{6,4},{5,7},{7,5},{8,10},{10,8},{9,1... | collective-permute-start | bytes 786440 | tf_op jit(solution)/shard_map/ppermute | solution.py:61
  138.5 2.9 %copy-start.20 = (f32[2,2,16,16,1]{2,3,0,1,4:T(8,128)S(1)}, f32[2,2,16,16,1]{2,3,0,1,4:T(8,128)}, u32[]{:S(2)}) copy-start(f32[2,2,16,16,1]{2,3,0,1,4:T(8,128)} %constant.81) | copy-start | bytes 12292
  141.4 2.8 %copy-start = (f32[16,128,2,128]{3,1,2,0:T(8,128)S(1)}, f32[16,128,2,128]{3,1,2,0:T(8,128)}, u32[]{:S(2)}) copy-start(f32[16,128,2,128]{3,1,2,0:T(8,128)} %get-tuple-element.17) | copy-start | bytes 6291460
  148.4 3.3 %copy-start.15 = (f32[1,32,16,128]{3,2,0,1:T(8,128)S(1)}, f32[1,32,16,128]{3,2,0,1:T(8,128)}, u32[]{:S(2)}) copy-start(f32[1,32,16,128]{3,2,0,1:T(8,128)} %get-tuple-element.28) | copy-start | bytes 786436
  148.4 3.4 %copy-start.14 = (f32[1,32,16,128]{3,2,0,1:T(8,128)S(1)}, f32[1,32,16,128]{3,2,0,1:T(8,128)}, u32[]{:S(2)}) copy-start(f32[1,32,16,128]{3,2,0,1:T(8,128)} %get-tuple-element.27) | copy-start | bytes 786436
  150.8 2.6 %copy-start.16 = (f32[1,32,16,128]{3,2,0,1:T(8,128)S(1)}, f32[1,32,16,128]{3,2,0,1:T(8,128)}, u32[]{:S(2)}) copy-start(f32[1,32,16,128]{3,2,0,1:T(8,128)} %get-tuple-element.25) | copy-start | bytes 786436
  160.1 1.8 %copy-start.5 = (f32[2,2,32,2048]{3,2,1,0:T(8,128)S(1)}, f32[2,2,32,2048]{3,2,1,0:T(8,128)}, u32[]{:S(2)}) copy-start(f32[2,2,32,2048]{3,2,1,0:T(8,128)} %get-tuple-element.16) | copy-start | bytes 3145732
  160.1 1.9 %copy-start.10 = (f32[4,8,16,128]{3,1,2,0:T(8,128)S(1)}, f32[4,8,16,128]{3,1,2,0:T(8,128)}, u32[]{:S(2)}) copy-start(f32[4,8,16,128]{3,1,2,0:T(8,128)} %copy.140) | copy-start | bytes 786436
  160.1 1.9 %copy-start.12 = (f32[4,8,16,128]{3,1,2,0:T(8,128)S(1)}, f32[4,8,16,128]{3,1,2,0:T(8,128)}, u32[]{:S(2)}) copy-start(f32[4,8,16,128]{3,1,2,0:T(8,128)} %copy.141) | copy-start | bytes 786436
  (7 other events, 11.0 us)
Sparse Core Ops, SparseCore 0:
  18.0 29.9 reduce-scatter.4
  50.4 25.7 reduce-scatter.6
  78.5 25.7 reduce-scatter.8
  106.5 25.7 reduce-scatter.10
